TPU v7x, 256 devices: a whole 4x4x8 slice. The times are simulated.
256 devices in a mesh: period: 128 (over z, x, y), half: 2 (over core).
Axes of the slice: x: 4, y: 4, z: 8, core: 2. Of those that a mesh axis runs over, the one named last changes fastest.
Arguments:
- probes: float32 [1024, 4, 512], P('period', None, 'half'), may hold values from -6 to 6
- footprints: bfloat16 [1024, 512, 512], P('period', None, 'half'), may hold values from -0.25 to 0.25
- lag_weights: float32 [1024, 4], P('period'), may hold values from 0.2 to 2
- owners: int32 [1024, 4], P('period'), may hold values from 0 to 127, all different within a row; in each aligned block of 8 rows (0 to 7, 8 to 15, ...) at most 2 rows name the same one
- window_tiles: int32 [1024, 2], P('period', 'half'), may hold values from 0 to 10
- coords: int32 [2, 3072], replicated, may hold values from 0 to 63
- temporal: float32 [128, 128], replicated, as said below
Outputs:
- coefficients: float32 [4, 4], replicated
- residual: float32 [1024, 4, 512], P('period', None, 'half')
Inputs may be any that keep to these rules, and one draw needn't show every extreme that they name: `owners`: each row names 4 different periods. Among the 8 rows of one index of period, no period is named more than 2 times, and one is named exactly 2 times. `temporal`: symmetric.
All inputs are finite; a program needn't handle non-finite values.
Results may differ from a plain program's by a relative error of at most 0.025.
Values may be sent and summed in bfloat16 or wider, within the bound.
No kernel may reach another device: no remote copies, remote signals or barrier semaphores. Data moves between devices by JAX's collectives and lax.ppermute only.
A program may use at most 64 MiB of HBM per device.

v0:
```python
import jax
import jax.numpy as jnp
from jax import lax
from jax.sharding import PartitionSpec as P

epsilon = 1e-06
kernel_scale = 0.05
kernel_length = 6.0
highest = lax.Precision.HIGHEST


def from_partner(block, axis, bit):
    count = lax.axis_size(axis)
    route = []
    for low in range(count):
        high = low | 1 << bit
        if high != low and high < count:
            route += [(low, high), (high, low)]
    return lax.ppermute(block, axis, route)


def body(probes, footprints, lag_weights, owners, window_tiles, coords, temporal):
    periods = lax.axis_size("period")
    half_index = lax.axis_index("half")
    block_count, top_count = owners.shape
    probe_count = probes.shape[1]
    sound_count = footprints.shape[1]
    window = footprints.shape[2]
    win_tiles = window // 128
    cell_count = coords.shape[1]
    half_cells = cell_count // 2
    tile_count = half_cells // 128
    group_cells = half_cells // periods
    total_rows = float(block_count * periods * sound_count)
    tiles = window_tiles[:, 0]
    tile_hot = (
        tiles[:, None, None] + jnp.arange(win_tiles, dtype=jnp.int32)[None, :, None]
        == jnp.arange(tile_count, dtype=jnp.int32)[None, None, :]
    ).astype(jnp.float32)
    own_coords = lax.dynamic_slice_in_dim(coords, half_index * half_cells, half_cells, 1)
    delta_x = own_coords[0][:, None] - coords[0][None, :]
    delta_y = own_coords[1][:, None] - coords[1][None, :]
    squared = (delta_x * delta_x + delta_y * delta_y).astype(jnp.float32)
    kernel_rows = (kernel_scale * jnp.exp(-jnp.sqrt(squared) / kernel_length)).reshape(
        periods, group_cells, cell_count
    )
    owner_hot = (owners[:, :, None] == jnp.arange(periods, dtype=jnp.int32)[None, None, :]).astype(
        jnp.float32
    )

    def add_half(piece_rows):
        return jnp.einsum(
            "bps,bsw->bpw", piece_rows, footprints, preferred_element_type=jnp.float32
        )

    def mix_periods(grouped_part):
        mixed_part = jnp.einsum("ts,sik->tik", temporal, grouped_part, precision=highest)
        return lax.all_to_all(mixed_part, "period", split_axis=0, concat_axis=0, tiled=True)

    def apply_operator(vector):
        vector_low = vector.astype(jnp.bfloat16)
        partial_value = add_half(lax.all_gather(vector_low, "half", axis=2, tiled=True))
        terms = lag_weights[:, :, None, None] * partial_value[:, None, :, :]
        term_tiles = terms.reshape(block_count, top_count, probe_count, win_tiles, 128)
        placed = jnp.einsum("bjt,bkpjl->bkptl", tile_hot, term_tiles, precision=highest)
        dense_terms = jnp.einsum("bkn,bkptl->nptl", owner_hot, placed, precision=highest)
        summed = lax.psum_scatter(
            dense_terms.reshape(periods, probe_count, half_cells),
            "period",
            scatter_dimension=0,
            tiled=True,
        )
        flux_half = summed[0]
        other_half = from_partner(flux_half, "half", 0)
        whole_flux = jnp.where(
            half_index == 0,
            jnp.concatenate([flux_half, other_half], axis=1),
            jnp.concatenate([other_half, flux_half], axis=1),
        )
        grouped = jnp.einsum("pc,gkc->gpk", whole_flux, kernel_rows, precision=highest)
        mixed_flux = mix_periods(
            lax.all_to_all(grouped, "period", split_axis=0, concat_axis=0, tiled=True)
        )
        field_low = (
            jnp.transpose(mixed_flux, (1, 0, 2))
            .reshape(probe_count, half_cells)
            .astype(jnp.bfloat16)
        )
        field_all = lax.all_gather(field_low[None], "period", axis=0, tiled=True)
        selected = jnp.einsum(
            "bkn,npc->bkpc",
            owner_hot.astype(jnp.bfloat16),
            field_all,
            preferred_element_type=jnp.float32,
        )
        selected = selected.reshape(block_count, top_count, probe_count, tile_count, 128)
        windows = jnp.einsum("bkptl,bjt->bkpjl", selected, tile_hot, precision=highest)
        windows = windows.astype(jnp.bfloat16).reshape(block_count, top_count, probe_count, window)
        products = jnp.einsum(
            "bkpw,bsw->bkps", windows, footprints, preferred_element_type=jnp.float32
        )
        sounded = jnp.einsum("bk,bkps->bps", lag_weights, products, precision=highest)
        return lax.psum_scatter(
            sounded.astype(jnp.bfloat16), "half", scatter_dimension=2, tiled=True
        ).astype(jnp.float32)

    def local_mean(values):
        return jnp.sum(values, axis=(0, 2))

    def lanczos_step(current, image):
        inner_sum = lax.psum(local_mean(current * image), ("period", "half"))
        alpha = inner_sum / total_rows
        remainder = image - alpha[None, :, None] * current
        square_sum = lax.psum(local_mean(remainder * remainder), ("period", "half"))
        beta = jnp.sqrt(square_sum / total_rows + epsilon)
        return (alpha, remainder, beta)

    start_sum = lax.psum(local_mean(probes * probes), ("period", "half"))
    first_q = probes / jnp.sqrt(start_sum / total_rows + epsilon)[None, :, None]
    image_one = apply_operator(first_q)
    alpha_one, rest_one, beta_one = lanczos_step(first_q, image_one)
    second_q = rest_one / beta_one[None, :, None]
    image_two = apply_operator(second_q) - beta_one[None, :, None] * first_q
    alpha_two, residual, beta_two = lanczos_step(second_q, image_two)
    coefficients = jnp.stack([alpha_one, beta_one, alpha_two, beta_two], axis=0)
    return (coefficients, residual)


def solution(mesh):
    in_specs = (
        P("period", None, "half"),
        P("period", None, "half"),
        P("period", None),
        P("period", None),
        P("period", "half"),
        P(),
        P(),
    )
    out_specs = (P(), P("period", None, "half"))
    return jax.shard_map(body, mesh=mesh, in_specs=in_specs, out_specs=out_specs, check_vma=False)
```

profile of v0, /device:TPU:1, one launch (start us, length us, event | category | flops | bytes accessed | tf_op | source)
XLA Modules:
  0.0 1305.8 jit_solution(13119377155676004425)
XLA Ops:
  8.3 81.4 %psum.35 = f32[4]{0:T(128)S(1)} all-reduce(f32[4]{0:T(128)S(1)} %multiply_reduce_fusion.3), channel_id=1, replica_groups=mesh['period'=128,'half'=2] {'period','half'}, use_global_device_ids=true, to_apply=%region_1.0 | all-reduce | flops 4 | bytes 32 | tf_op jit(solution)/shard_map/psum | solution.py:118
  92.0 2.5 all_gather.12
  95.7 4.4 fusion.38
  100.1 5.1 copy.26
  106.4 221.5 %all-reduce.5.cloned.1.call-done = f32[128,4,1536]{2,1,0:T(4,128)} async-done(((f32[128,4,1536]{2,1,0:T(4,128)}), f32[128,4,1536]{2,1,0:T(4,128)}) %all-reduce.5.cloned.1.call-update) | async-done | bytes 3145744
  329.4 4.9 collective-permute-start
  335.2 46.6 %fusion.32 = f32[128,4,12]{0,1,2:T(4,128)S(1)} fusion(s32[3072]{0:T(1024)S(1)} %bitcast.132, s32[128,12]{0,1:T(8,128)S(1)} %copy.23, s32[3072]{0:T(1024)S(1)} %bitcast.130, s32[128,12]{0,1:T(8,128)S(1)} %copy.22, f32[4,1536]{1,0:T(4,128)S(1)} %collective-permute-done, f32[4,1536]{1,0:T(4,128)S(1)} %dynamic-slice_bitcast_fusion.1, pred[]{:T(512)S(6)} %eq.36), kind=kOutput, calls=%fused_computation.35 | convolution fusion | flops 268996608 | bytes 110593 | tf_op jit(solution)/shard_map/pc,gkc->gpk/dot_general | solution.py:80
  382.0 23.7 %all_to_all.20 = f32[128,4,12]{2,1,0:T(4,128)S(1)} all-to-all(f32[128,4,12]{2,1,0:T(4,128)S(1)} %copy.27), channel_id=1, replica_groups=mesh['period'=128,'half'=2] {'period'}, dimensions={0} | all-to-all | bytes 49152 | tf_op jit(solution)/shard_map/all_to_all | solution.py:82
  406.4 17.2 %all_to_all.21 = bf16[128,4,12]{2,1,0:T(4,128)(2,1)S(1)} all-to-all(bf16[128,4,12]{2,1,0:T(4,128)(2,1)S(1)} %copy.29), channel_id=1, replica_groups=mesh['period'=128,'half'=2] {'period'}, dimensions={0} | all-to-all | bytes 24576 | tf_op jit(solution)/shard_map/all_to_all | solution.py:58
  424.8 94.2 %all-gather.3.cloned.1.call-done = bf16[128,4,1536]{2,1,0:T(4,128)(2,1)} async-done(((bf16[1,4,1536]{2,1,0:T(4,128)(2,1)}), bf16[128,4,1536]{2,1,0:T(4,128)(2,1)}) %all-gather.3.cloned.1.call-update) | async-done | bytes 1572880 | tf_op jit(solution)/shard_map/all_gather | solution.py:89
  525.1 16.9 %reduce-scatter.7.cloned.1.call-done = bf16[256,32]{1,0:T(8,128)(2,1)} async-done(((bf16[512,32]{1,0:T(8,128)(2,1)}), bf16[256,32]{1,0:T(8,128)(2,1)}) %reduce-scatter.7.cloned.1.call-update) | async-done | bytes 16400
  543.7 77.4 %psum.36 = f32[4]{0:T(128)S(1)} all-reduce(f32[4]{0:T(128)S(1)} %fusion.68), channel_id=1, replica_groups=mesh['period'=128,'half'=2] {'period','half'}, use_global_device_ids=true, to_apply=%region_5.6 | all-reduce | flops 4 | bytes 32 | tf_op jit(solution)/shard_map/psum | solution.py:111
  621.3 73.1 %psum.37 = f32[4]{0:T(128)S(1)} all-reduce(f32[4]{0:T(128)S(1)} %multiply_reduce_fusion.2), channel_id=1, replica_groups=mesh['period'=128,'half'=2] {'period','half'}, use_global_device_ids=true, to_apply=%region_7.8 | all-reduce | flops 4 | bytes 32 | tf_op jit(solution)/shard_map/psum | solution.py:114
  697.9 4.4 fusion.36
  702.3 5.1 copy.34
  707.5 223.8 %all-reduce.7.cloned.1.call-done = f32[128,4,1536]{2,1,0:T(4,128)} async-done(((f32[128,4,1536]{2,1,0:T(4,128)}), f32[128,4,1536]{2,1,0:T(4,128)}) %all-reduce.7.cloned.1.call-update) | async-done | bytes 3145744
  932.7 4.9 collective-permute-start.1
  938.5 46.6 %fusion.33 = f32[128,4,12]{0,1,2:T(4,128)S(1)} fusion(s32[3072]{0:T(1024)S(1)} %bitcast.133, s32[128,12]{0,1:T(8,128)S(1)} %copy.23, s32[3072]{0:T(1024)S(1)} %bitcast.131, s32[128,12]{0,1:T(8,128)S(1)} %copy.22, f32[4,1536]{1,0:T(4,128)S(1)} %collective-permute-done.1, f32[4,1536]{1,0:T(4,128)S(1)} %dynamic-slice_bitcast_fusion, pred[]{:T(512)S(6)} %eq.36), kind=kOutput, calls=%fused_computation.36 | convolution fusion | flops 268996608 | bytes 110593 | tf_op jit(solution)/shard_map/pc,gkc->gpk/dot_general | solution.py:80
  985.3 23.7 %all_to_all.22 = f32[128,4,12]{2,1,0:T(4,128)S(1)} all-to-all(f32[128,4,12]{2,1,0:T(4,128)S(1)} %copy.35), channel_id=1, replica_groups=mesh['period'=128,'half'=2] {'period'}, dimensions={0} | all-to-all | bytes 49152 | tf_op jit(solution)/shard_map/all_to_all | solution.py:82
  1009.7 17.2 %all_to_all.23 = bf16[128,4,12]{2,1,0:T(4,128)(2,1)S(1)} all-to-all(bf16[128,4,12]{2,1,0:T(4,128)(2,1)S(1)} %copy.37), channel_id=1, replica_groups=mesh['period'=128,'half'=2] {'period'}, dimensions={0} | all-to-all | bytes 24576 | tf_op jit(solution)/shard_map/all_to_all | solution.py:58
  1027.9 94.5 %all-gather.5.cloned.1.call-done = bf16[128,4,1536]{2,1,0:T(4,128)(2,1)} async-done(((bf16[1,4,1536]{2,1,0:T(4,128)(2,1)}), bf16[128,4,1536]{2,1,0:T(4,128)(2,1)}) %all-gather.5.cloned.1.call-update) | async-done | bytes 1572880 | tf_op jit(solution)/shard_map/all_gather | solution.py:89
  1128.4 16.9 %reduce-scatter.9.cloned.1.call-done = bf16[256,32]{1,0:T(8,128)(2,1)} async-done(((bf16[512,32]{1,0:T(8,128)(2,1)}), bf16[256,32]{1,0:T(8,128)(2,1)}) %reduce-scatter.9.cloned.1.call-update) | async-done | bytes 16400
  1147.0 77.4 %psum.38 = f32[4]{0:T(128)S(1)} all-reduce(f32[4]{0:T(128)S(1)} %multiply_reduce_fusion.1), channel_id=1, replica_groups=mesh['period'=128,'half'=2] {'period','half'}, use_global_device_ids=true, to_apply=%region_11.12 | all-reduce | flops 4 | bytes 32 | tf_op jit(solution)/shard_map/psum | solution.py:111
  1225.3 73.1 %psum.39 = f32[4]{0:T(128)S(1)} all-reduce(f32[4]{0:T(128)S(1)} %get-tuple-element.4), channel_id=1, replica_groups=mesh['period'=128,'half'=2] {'period','half'}, use_global_device_ids=true, to_apply=%region_13.14 | all-reduce | flops 4 | bytes 32 | tf_op jit(solution)/shard_map/psum | solution.py:114
  (88 shorter events, 34.7 us)
Async XLA Ops:
  7.2 87.3 %copy-start = (bf16[8,512,256]{2,1,0:T(8,128)(2,1)S(1)}, bf16[8,512,256]{2,1,0:T(8,128)(2,1)}, u32[]{:S(2)}) copy-start(bf16[8,512,256]{2,1,0:T(8,128)(2,1)} %param.8) | copy-start | bytes 6291460
  7.2 88.5 %copy-start.3 = (s32[8,4]{0,1:T(4,128)S(1)}, s32[8,4]{0,1:T(4,128)}, u32[]{:S(2)}) copy-start(s32[8,4]{0,1:T(4,128)} %param.10) | copy-start | bytes 388
  7.2 320.8 %all-reduce.5.cloned.1.call-start = ((), (), s32[]{:S(2)}) async-start(), calls=%async_computation.10 | async-start | bytes 6291456
  105.2 0.7 copy-start.5
  105.2 229.1 %copy-start.2 = (s32[2,3072]{1,0:T(2,128)S(1)}, s32[2,3072]{1,0:T(2,128)}, u32[]{:S(2)}) copy-start(s32[2,3072]{1,0:T(2,128)} %param.12) | copy-start | bytes 73732
  105.2 413.8 %all-gather.3.cloned.1.call-start = ((), (), s32[]{:S(2)}) async-start(), calls=%async_computation.6 | async-start | bytes 1585152 | tf_op jit(solution)/shard_map/all_gather | solution.py:89
  329.4 5.8 collective-permute-start
  335.2 70.5 %copy-start.1 = (f32[128,128]{1,0:T(8,128)S(1)}, f32[128,128]{1,0:T(8,128)}, u32[]{:S(2)}) copy-start(f32[128,128]{1,0:T(8,128)} %param.13) | copy-start | bytes 196612
  335.2 89.6 %copy-start.4 = (f32[8,4]{0,1:T(4,128)S(1)}, f32[8,4]{0,1:T(4,128)}, u32[]{:S(2)}) copy-start(f32[8,4]{0,1:T(4,128)} %param.9) | copy-start | bytes 388
  424.5 117.5 %reduce-scatter.7.cloned.1.call-start = ((), (), s32[]{:S(2)}) async-start(), calls=%async_computation.8 | async-start | bytes 196608
  525.0 406.2 %all-reduce.7.cloned.1.call-start = ((), (), s32[]{:S(2)}) async-start(), calls=%async_computation.11 | async-start | bytes 6291456
  707.4 414.9 %all-gather.5.cloned.1.call-start = ((), (), s32[]{:S(2)}) async-start(), calls=%async_computation.7 | async-start | bytes 1585152 | tf_op jit(solution)/shard_map/all_gather | solution.py:89
  932.7 5.8 collective-permute-start.1
  1027.8 117.5 %reduce-scatter.9.cloned.1.call-start = ((), (), s32[]{:S(2)}) async-start(), calls=%async_computation.9 | async-start | bytes 196608
Sparse Core Ops, SparseCore 0:
  105.3 222.5 all-reduce.4
  424.6 94.3 all-gather.2
  525.2 16.7 reduce-scatter.6
  707.5 223.6 all-reduce.6
  1027.9 94.3 all-gather.4
  1128.5 16.7 reduce-scatter.8
where the time goes:
time: 1310 us
  waiting for transfers between devices  669 us (51%)
  blocking collectives  469 us (36%)
  matrix products  113 us (9%)
  local copies, waits for them, and re-layouts  25.2 us (2%)
  between operations  14.4 us (1%)
    unnamed x10, waiting for transfers between devices  479 us
    all_gather x2, waiting for transfers between devices, apply_operator(): field_all = lax.all_gather(field_low[None], 'period', axis=0, tiled=True)  189 us
    psum x2, blocking collectives, lanczos_step(): inner_sum = lax.psum(local_mean(current * image), ('period', 'half'))  155 us
    psum x2, blocking collectives, lanczos_step(): square_sum = lax.psum(local_mean(remainder * remainder), ('period', 'half'))  146 us
    dot_general x2, matrix products, apply_operator(): jnp.einsum('pc,gkc->gpk', whole_flux, kernel_rows, precision=highest)  93.3 us
    psum x1, blocking collectives, body(): start_sum = lax.psum(local_mean(probes * probes), ('period', 'half'))  81.4 us
    all_to_all x2, blocking collectives, apply_operator(): lax.all_to_all(grouped, 'period', split_axis=0, concat_axis=0, tiled=True)  47.4 us
    all_to_all x2, blocking collectives, mix_periods(): lax.all_to_all(mixed_part, 'period', split_axis=0, concat_axis=0, tiled=T...  34.5 us
  transfers between devices with their start and end apart: 8, of which 8 were waited for; matrix products, arithmetic and copies ran while one was open for 0% of the time, Pallas kernels for 0%

commit v1 on v0

--- a/solution.py
+++ b/solution.py
@@ -115,7 +115,7 @@
         beta = jnp.sqrt(square_sum / total_rows + epsilon)
         return (alpha, remainder, beta)
 
-    start_sum = lax.psum(local_mean(probes * probes), ("period", "half"))
+    start_sum = lax.psum(lax.psum(local_mean(probes * probes), "half"), "period")
     first_q = probes / jnp.sqrt(start_sum / total_rows + epsilon)[None, :, None]
     image_one = apply_operator(first_q)
     alpha_one, rest_one, beta_one = lanczos_step(first_q, image_one)

time: 1310 us -> 1580 us (1.21)
  blocking collectives: 469 us -> 743 us
    psum x1 -> x2, blocking collectives: 81.4 us -> 301 us  [the longest x1 296 us: body(): lax.psum(lax.psum(local_mean(probes * probes), 'half'), 'period')]
    all_gather x2, blocking collectives: 4.65 us -> 59.3 us  [apply_operator(): lax.all_gather(vector_low, 'half', axis=2, tiled=True)]
where the time goes in v1:
time: 1580 us
  blocking collectives  743 us (47%)
  waiting for transfers between devices  666 us (42%)
  matrix products  113 us (7%)
  local copies, waits for them, and re-layouts  25.2 us (2%)
    unnamed x10, waiting for transfers between devices  476 us
    psum x1, blocking collectives, body(): lax.psum(lax.psum(local_mean(probes * probes), 'half'), 'period')  296 us
    all_gather x2, waiting for transfers between devices, apply_operator(): field_all = lax.all_gather(field_low[None], 'period', axis=0, tiled=True)  189 us
    psum x2, blocking collectives, lanczos_step(): inner_sum = lax.psum(local_mean(current * image), ('period', 'half'))  155 us
    psum x2, blocking collectives, lanczos_step(): square_sum = lax.psum(local_mean(remainder * remainder), ('period', 'half'))  146 us
    dot_general x2, matrix products, apply_operator(): jnp.einsum('pc,gkc->gpk', whole_flux, kernel_rows, precision=highest)  93.3 us
    all_gather x2, blocking collectives, apply_operator(): lax.all_gather(vector_low, 'half', axis=2, tiled=True)  59.3 us
    all_to_all x2, blocking collectives, apply_operator(): lax.all_to_all(grouped, 'period', split_axis=0, concat_axis=0, tiled=True)  47.4 us
  transfers between devices with their start and end apart: 8, of which 8 were waited for; matrix products, arithmetic and copies ran while one was open for 0% of the time, Pallas kernels for 0%

profile of v1, /device:TPU:1, one launch (start us, length us, event | category | flops | bytes accessed | tf_op | source)
XLA Modules:
  0.0 1577.1 jit_solution(17781988904346557545)
XLA Ops:
  8.3 5.3 psum.42
  13.6 295.7 %psum.43 = f32[4]{0:T(128)S(1)} all-reduce(f32[4]{0:T(128)S(1)} %psum.42), channel_id=1, replica_groups=mesh['period'=128,'half'=2] {'period'}, use_global_device_ids=true, to_apply=%region_2.0 | all-reduce | flops 4 | bytes 32 | tf_op jit(solution)/shard_map/psum | solution.py:118
  311.7 57.1 %all_gather.12 = bf16[8,4,512]{2,1,0:T(4,128)(2,1)S(1)} all-gather(bf16[8,4,256]{2,1,0:T(4,128)(2,1)S(1)} %get-tuple-element.8), channel_id=1, replica_groups=mesh['period'=128,'half'=2] {'half'}, dimensions={2}, use_global_device_ids=true | all-gather | bytes 49152 | tf_op jit(solution)/shard_map/all_gather | solution.py:62
  370.0 4.4 fusion.38
  374.3 5.1 copy.26
  380.7 218.5 %all-reduce.5.cloned.1.call-done = f32[128,4,1536]{2,1,0:T(4,128)} async-done(((f32[128,4,1536]{2,1,0:T(4,128)}), f32[128,4,1536]{2,1,0:T(4,128)}) %all-reduce.5.cloned.1.call-update) | async-done | bytes 3145744
  600.6 4.9 collective-permute-start
  606.4 46.6 %fusion.32 = f32[128,4,12]{0,1,2:T(4,128)S(1)} fusion(s32[3072]{0:T(1024)S(1)} %bitcast.132, s32[128,12]{0,1:T(8,128)S(1)} %copy.23, s32[3072]{0:T(1024)S(1)} %bitcast.130, s32[128,12]{0,1:T(8,128)S(1)} %copy.22, f32[4,1536]{1,0:T(4,128)S(1)} %collective-permute-done, f32[4,1536]{1,0:T(4,128)S(1)} %dynamic-slice_bitcast_fusion.1, pred[]{:T(512)S(6)} %eq.36), kind=kOutput, calls=%fused_computation.35 | convolution fusion | flops 268996608 | bytes 110593 | tf_op jit(solution)/shard_map/pc,gkc->gpk/dot_general | solution.py:80
  653.3 23.7 %all_to_all.20 = f32[128,4,12]{2,1,0:T(4,128)S(1)} all-to-all(f32[128,4,12]{2,1,0:T(4,128)S(1)} %copy.27), channel_id=1, replica_groups=mesh['period'=128,'half'=2] {'period'}, dimensions={0} | all-to-all | bytes 49152 | tf_op jit(solution)/shard_map/all_to_all | solution.py:82
  677.7 17.2 %all_to_all.21 = bf16[128,4,12]{2,1,0:T(4,128)(2,1)S(1)} all-to-all(bf16[128,4,12]{2,1,0:T(4,128)(2,1)S(1)} %copy.29), channel_id=1, replica_groups=mesh['period'=128,'half'=2] {'period'}, dimensions={0} | all-to-all | bytes 24576 | tf_op jit(solution)/shard_map/all_to_all | solution.py:58
  696.1 94.2 %all-gather.3.cloned.1.call-done = bf16[128,4,1536]{2,1,0:T(4,128)(2,1)} async-done(((bf16[1,4,1536]{2,1,0:T(4,128)(2,1)}), bf16[128,4,1536]{2,1,0:T(4,128)(2,1)}) %all-gather.3.cloned.1.call-update) | async-done | bytes 1572880 | tf_op jit(solution)/shard_map/all_gather | solution.py:89
  796.4 16.9 %reduce-scatter.7.cloned.1.call-done = bf16[256,32]{1,0:T(8,128)(2,1)} async-done(((bf16[512,32]{1,0:T(8,128)(2,1)}), bf16[256,32]{1,0:T(8,128)(2,1)}) %reduce-scatter.7.cloned.1.call-update) | async-done | bytes 16400
  815.0 77.4 %psum.44 = f32[4]{0:T(128)S(1)} all-reduce(f32[4]{0:T(128)S(1)} %fusion.68), channel_id=1, replica_groups=mesh['period'=128,'half'=2] {'period','half'}, use_global_device_ids=true, to_apply=%region_6.7 | all-reduce | flops 4 | bytes 32 | tf_op jit(solution)/shard_map/psum | solution.py:111
  892.6 73.1 %psum.45 = f32[4]{0:T(128)S(1)} all-reduce(f32[4]{0:T(128)S(1)} %multiply_reduce_fusion.2), channel_id=1, replica_groups=mesh['period'=128,'half'=2] {'period','half'}, use_global_device_ids=true, to_apply=%region_8.9 | all-reduce | flops 4 | bytes 32 | tf_op jit(solution)/shard_map/psum | solution.py:114
  973.6 5.1 copy.34
  978.8 223.8 %all-reduce.7.cloned.1.call-done = f32[128,4,1536]{2,1,0:T(4,128)} async-done(((f32[128,4,1536]{2,1,0:T(4,128)}), f32[128,4,1536]{2,1,0:T(4,128)}) %all-reduce.7.cloned.1.call-update) | async-done | bytes 3145744
  1204.0 4.9 collective-permute-start.1
  1209.8 46.6 %fusion.33 = f32[128,4,12]{0,1,2:T(4,128)S(1)} fusion(s32[3072]{0:T(1024)S(1)} %bitcast.133, s32[128,12]{0,1:T(8,128)S(1)} %copy.23, s32[3072]{0:T(1024)S(1)} %bitcast.131, s32[128,12]{0,1:T(8,128)S(1)} %copy.22, f32[4,1536]{1,0:T(4,128)S(1)} %collective-permute-done.1, f32[4,1536]{1,0:T(4,128)S(1)} %dynamic-slice_bitcast_fusion, pred[]{:T(512)S(6)} %eq.36), kind=kOutput, calls=%fused_computation.36 | convolution fusion | flops 268996608 | bytes 110593 | tf_op jit(solution)/shard_map/pc,gkc->gpk/dot_general | solution.py:80
  1256.6 23.7 %all_to_all.22 = f32[128,4,12]{2,1,0:T(4,128)S(1)} all-to-all(f32[128,4,12]{2,1,0:T(4,128)S(1)} %copy.35), channel_id=1, replica_groups=mesh['period'=128,'half'=2] {'period'}, dimensions={0} | all-to-all | bytes 49152 | tf_op jit(solution)/shard_map/all_to_all | solution.py:82
  1281.0 17.2 %all_to_all.23 = bf16[128,4,12]{2,1,0:T(4,128)(2,1)S(1)} all-to-all(bf16[128,4,12]{2,1,0:T(4,128)(2,1)S(1)} %copy.37), channel_id=1, replica_groups=mesh['period'=128,'half'=2] {'period'}, dimensions={0} | all-to-all | bytes 24576 | tf_op jit(solution)/shard_map/all_to_all | solution.py:58
  1299.2 94.5 %all-gather.5.cloned.1.call-done = bf16[128,4,1536]{2,1,0:T(4,128)(2,1)} async-done(((bf16[1,4,1536]{2,1,0:T(4,128)(2,1)}), bf16[128,4,1536]{2,1,0:T(4,128)(2,1)}) %all-gather.5.cloned.1.call-update) | async-done | bytes 1572880 | tf_op jit(solution)/shard_map/all_gather | solution.py:89
  1399.7 16.9 %reduce-scatter.9.cloned.1.call-done = bf16[256,32]{1,0:T(8,128)(2,1)} async-done(((bf16[512,32]{1,0:T(8,128)(2,1)}), bf16[256,32]{1,0:T(8,128)(2,1)}) %reduce-scatter.9.cloned.1.call-update) | async-done | bytes 16400
  1418.4 77.4 %psum.46 = f32[4]{0:T(128)S(1)} all-reduce(f32[4]{0:T(128)S(1)} %multiply_reduce_fusion.1), channel_id=1, replica_groups=mesh['period'=128,'half'=2] {'period','half'}, use_global_device_ids=true, to_apply=%region_12.13 | all-reduce | flops 4 | bytes 32 | tf_op jit(solution)/shard_map/psum | solution.py:111
  1496.6 73.1 %psum.47 = f32[4]{0:T(128)S(1)} all-reduce(f32[4]{0:T(128)S(1)} %get-tuple-element.4), channel_id=1, replica_groups=mesh['period'=128,'half'=2] {'period','half'}, use_global_device_ids=true, to_apply=%region_14.15 | all-reduce | flops 4 | bytes 32 | tf_op jit(solution)/shard_map/psum | solution.py:114
  (89 shorter events, 39.1 us)
Async XLA Ops:
  7.2 361.6 %copy-start = (bf16[8,512,256]{2,1,0:T(8,128)(2,1)S(1)}, bf16[8,512,256]{2,1,0:T(8,128)(2,1)}, u32[]{:S(2)}) copy-start(bf16[8,512,256]{2,1,0:T(8,128)(2,1)} %param.8) | copy-start | bytes 6291460
  7.2 362.8 %copy-start.3 = (s32[8,4]{0,1:T(4,128)S(1)}, s32[8,4]{0,1:T(4,128)}, u32[]{:S(2)}) copy-start(s32[8,4]{0,1:T(4,128)} %param.10) | copy-start | bytes 388
  7.2 592.1 %all-reduce.5.cloned.1.call-start = ((), (), s32[]{:S(2)}) async-start(), calls=%async_computation.10 | async-start | bytes 6291456
  379.5 0.7 copy-start.5
  379.5 226.1 %copy-start.2 = (s32[2,3072]{1,0:T(2,128)S(1)}, s32[2,3072]{1,0:T(2,128)}, u32[]{:S(2)}) copy-start(s32[2,3072]{1,0:T(2,128)} %param.12) | copy-start | bytes 73732
  379.5 410.8 %all-gather.3.cloned.1.call-start = ((), (), s32[]{:S(2)}) async-start(), calls=%async_computation.6 | async-start | bytes 1585152 | tf_op jit(solution)/shard_map/all_gather | solution.py:89
  600.6 5.8 collective-permute-start
  606.4 70.5 %copy-start.1 = (f32[128,128]{1,0:T(8,128)S(1)}, f32[128,128]{1,0:T(8,128)}, u32[]{:S(2)}) copy-start(f32[128,128]{1,0:T(8,128)} %param.13) | copy-start | bytes 196612
  606.4 89.6 %copy-start.4 = (f32[8,4]{0,1:T(4,128)S(1)}, f32[8,4]{0,1:T(4,128)}, u32[]{:S(2)}) copy-start(f32[8,4]{0,1:T(4,128)} %param.9) | copy-start | bytes 388
  695.8 117.5 %reduce-scatter.7.cloned.1.call-start = ((), (), s32[]{:S(2)}) async-start(), calls=%async_computation.8 | async-start | bytes 196608
  796.3 406.3 %all-reduce.7.cloned.1.call-start = ((), (), s32[]{:S(2)}) async-start(), calls=%async_computation.11 | async-start | bytes 6291456
  978.7 414.9 %all-gather.5.cloned.1.call-start = ((), (), s32[]{:S(2)}) async-start(), calls=%async_computation.7 | async-start | bytes 1585152 | tf_op jit(solution)/shard_map/all_gather | solution.py:89
  1204.0 5.8 collective-permute-start.1
  1299.1 117.5 %reduce-scatter.9.cloned.1.call-start = ((), (), s32[]{:S(2)}) async-start(), calls=%async_computation.9 | async-start | bytes 196608
Sparse Core Ops, SparseCore 0:
  379.6 219.6 all-reduce.4
  695.9 94.3 all-gather.2
  796.5 16.7 reduce-scatter.6
  978.8 223.7 all-reduce.6
  1299.2 94.3 all-gather.4
  1399.8 16.7 reduce-scatter.8
